TPU v7x, 32 devices: a whole 2x2x4 slice. The times are simulated.
32 devices in a mesh: wide: 8 (over y, x, core), narrow: 4 (over z).
Axes of the slice: x: 2, y: 2, z: 4, core: 2. Of those that a mesh axis runs over, the one named last changes fastest.
Arguments:
- positions: float32 [3, 4096], P(None, ('wide', 'narrow')), may hold values from 0 to 8, as said below
- features: float32 [4096, 256], P(('wide', 'narrow')), may hold values from -6 to 6
- block_counts: int32 [8], P('wide'), may hold values from 2 to 4, as said below
- pair_list: int32 [8, 4, 3, 4], P('wide', 'narrow'), may hold values from 0 to 3, as said below
- pair_count: int32 [8, 4], P('wide', 'narrow'), may hold values from 0 to 4, as said below
- pair_mask: int32 [8, 4, 4, 128, 128], P('wide', 'narrow'), may hold values 0 or 1
- w_rbf: float32 [16, 256], replicated, may hold values from -0.125 to 0.125
- wavevectors: float32 [3, 2048], P(None, 'narrow'), may hold values from -3 to 3
- kfilter: float32 [2048, 256], P('narrow'), may hold values from 1 to 30
- w_in: bfloat16 [256, 512], replicated, may hold values from -0.375 to 0.375
- w_out: bfloat16 [512, 256], replicated, may hold values from -0.25 to 0.25
Outputs:
- updated: float32 [4096, 256], P(('wide', 'narrow'))
Inputs may be any that keep to these rules, and one draw needn't show every extreme that they name: `positions`: atoms of slab s have their first coordinate in [s, s + 1), the other two in [0, 1). The live blocks of a slab are its first block_counts ones; some slab and the next one both hold 4 live blocks. `pair_list`: slots below pair_count of a device are valid, the rest hold zeros. Row 0 is a local block of the device (below 1), row 1 the slab offset (0: own slab, 1: next slab), row 2 a block of that slab (below 4); both blocks are live; with offset 0 the peer block's index in the slab is greater than the own block's; each unordered block pair appears in at most one valid slot of all devices. `pair_count`: some device lists 4 pairs.
All inputs are finite; a program needn't handle non-finite values. No bound on the sum of `pair_mask` on one device may be relied on, other than what follows from the above.
Results may differ from a plain program's by a relative error of at most 0.005.
Values sent between devices are 32-bit elements; how exact they have to be, the bound alone decides.
A program may use at most 64 MiB of HBM per device.

v0:
```python
import jax
import jax.numpy as jnp
from jax import lax
from jax.sharding import PartitionSpec as P

RBF = 16
BLOCK = 128


cutoff = 2.0
sigma_width = 0.25


def from_behind(shard, axis, by):
    count = lax.axis_size(axis)
    pairs = [(i, i + by) for i in range(count) if 0 <= i + by < count]
    return lax.ppermute(shard, axis, pairs)


def radial_filters(own_pos, peer_pos, mask_values):
    delta_x = own_pos[0][:, None] - peer_pos[0][None, :]
    delta_y = own_pos[1][:, None] - peer_pos[1][None, :]
    delta_z = own_pos[2][:, None] - peer_pos[2][None, :]
    squared = delta_x * delta_x + delta_y * delta_y + delta_z * delta_z
    distance = jnp.sqrt(squared + 0.01)
    centers = jnp.arange(RBF, dtype=jnp.float32) * (cutoff / (RBF - 1))
    envelope = (1.0 - jnp.minimum(squared / (cutoff * cutoff), 1.0)) ** 2
    scaled = (distance[:, None, :] - centers[None, :, None]) / sigma_width
    return (jnp.exp(-scaled * scaled) * (envelope * mask_values)[:, None, :]).astype(jnp.bfloat16)


def local(
    positions,
    features,
    block_counts,
    pair_list,
    pair_count,
    pair_mask,
    w_rbf,
    wavevectors,
    kfilter,
    w_in,
    w_out,
):
    atoms_dev = features.shape[0]
    channels = features.shape[1]
    narrow_index = lax.axis_index("narrow")
    slab_pos, slab_feat = (
        lax.all_gather(positions, "narrow", axis=1, tiled=True),
        lax.all_gather(features, "narrow", axis=0, tiled=True),
    )
    next_pos, next_feat = from_behind((slab_pos, slab_feat), "wide", -1)
    slab_atoms = slab_feat.shape[0]
    live_count = block_counts[0]
    slab_live = (jnp.arange(slab_atoms) // BLOCK < live_count).astype(jnp.float32)
    own_live = lax.dynamic_slice_in_dim(slab_live, narrow_index * atoms_dev, atoms_dev, 0)
    phases = (
        wavevectors[0][:, None] * slab_pos[0][None, :]
        + wavevectors[1][:, None] * slab_pos[1][None, :]
        + wavevectors[2][:, None] * slab_pos[2][None, :]
    )
    tables = jnp.concatenate([jnp.cos(phases), jnp.sin(phases)], axis=0).astype(jnp.bfloat16)
    weighted = (slab_feat * slab_live[:, None]).astype(jnp.bfloat16)
    partial_value = jnp.dot(tables, weighted, preferred_element_type=jnp.float32)
    factors = lax.psum(partial_value, "wide")
    atoms_all = slab_atoms * lax.axis_size("wide")
    filtered = (jnp.concatenate([kfilter, kfilter], axis=0) * factors / atoms_all).astype(
        jnp.bfloat16
    )
    long_part = lax.dot_general(
        tables, filtered, (((0,), (0,)), ((), ())), preferred_element_type=jnp.float32
    )
    both_pos = jnp.stack([slab_pos, next_pos])
    both_feat = jnp.stack([slab_feat, next_feat])
    slot_masks = pair_mask[0, 0]
    listing = pair_list[0, 0]
    listed = pair_count[0, 0]
    anchor = jnp.int32(0)

    def add_pair(slot_index, buffers):
        local_block = listing[0, slot_index]
        offset = listing[1, slot_index]
        peer_block = listing[2, slot_index]
        own_start = local_block * BLOCK
        slab_start = narrow_index * atoms_dev + own_start
        peer_start = peer_block * BLOCK
        peer_pos = lax.dynamic_slice(both_pos, (offset, anchor, peer_start), (1, 3, BLOCK))[0]
        peer_feat = lax.dynamic_slice(
            both_feat, (offset, peer_start, anchor), (1, BLOCK, channels)
        )[0]
        filters = radial_filters(positions, peer_pos, slot_masks[slot_index].astype(jnp.float32))
        peer_terms = (
            (peer_feat[None] * w_rbf[:, None, :])
            .astype(jnp.bfloat16)
            .reshape(RBF * BLOCK, channels)
        )
        own_terms = (features[None] * w_rbf[:, None, :]).astype(jnp.bfloat16)
        to_own = jnp.dot(
            filters.reshape(BLOCK, RBF * BLOCK), peer_terms, preferred_element_type=jnp.float32
        )
        to_peer = jnp.einsum("akb,kac->bc", filters, own_terms, preferred_element_type=jnp.float32)
        current = lax.dynamic_slice(buffers, (anchor, slab_start, anchor), (1, BLOCK, channels))
        buffers = lax.dynamic_update_slice(
            buffers, current + to_own[None], (anchor, slab_start, anchor)
        )
        current = lax.dynamic_slice(buffers, (offset, peer_start, anchor), (1, BLOCK, channels))
        return lax.dynamic_update_slice(
            buffers, current + to_peer[None], (offset, peer_start, anchor)
        )

    buffers = lax.fori_loop(0, listed, add_pair, jnp.zeros((2, slab_atoms, channels), jnp.float32))
    arrived = from_behind(buffers[1], "wide", 1)
    own_rows = lax.psum_scatter(
        buffers[0] + arrived + long_part, "narrow", scatter_dimension=0, tiled=True
    )
    message = own_rows.astype(jnp.bfloat16)
    hidden = jax.nn.silu(jnp.dot(message, w_in, preferred_element_type=jnp.float32)).astype(
        jnp.bfloat16
    )
    return own_live[:, None] * (
        features + jnp.dot(hidden, w_out, preferred_element_type=jnp.float32)
    )


def solution(mesh):
    placed = (
        P(None, ("wide", "narrow")),
        P(("wide", "narrow"), None),
        P("wide"),
        P("wide", "narrow", None, None),
        P("wide", "narrow"),
        P("wide", "narrow", None, None, None),
        P(),
        P(None, "narrow"),
        P("narrow", None),
        P(),
        P(),
    )
    return jax.shard_map(
        local, mesh=mesh, in_specs=placed, out_specs=P(("wide", "narrow"), None), check_vma=False
    )
```

profile of v0, /device:TPU:0, one launch (start us, length us, event | category | flops | bytes accessed | tf_op | source)
XLA Modules:
  0.0 141.9 jit_solution(6122852817616642391)
XLA Ops:
  6.5 13.9 %all_gather.6 = f32[3,512]{1,0:T(4,128)S(1)} all-gather(f32[3,128]{1,0:T(4,128)} %param.13), channel_id=1, replica_groups=mesh['wide'=8,'narrow'=4] {'narrow'}, dimensions={1}, use_global_device_ids=true | all-gather | bytes 7680 | tf_op jit(solution)/shard_map/all_gather | solution.py:49
  20.4 1.3 collective-permute-start
  21.7 16.1 %all_gather.7 = f32[512,256]{1,0:T(8,128)S(1)} all-gather(f32[128,256]{1,0:T(8,128)} %param.14), channel_id=1, replica_groups=mesh['wide'=8,'narrow'=4] {'narrow'}, dimensions={0}, use_global_device_ids=true | all-gather | bytes 655360 | tf_op jit(solution)/shard_map/all_gather | solution.py:50
  37.8 1.3 collective-permute-start.1
  39.1 0.8 fusion.43
  40.0 4.5 %cosine_convert_fusion = (bf16[512,512]{1,0:T(8,128)(2,1)S(1)}, bf16[512,512]{1,0:T(8,128)(2,1)S(1)}) fusion(f32[512]{0:T(512)S(1)} %bitcast.80, f32[512]{0:T(512)S(1)} %bitcast.83, f32[512]{0:T(512)S(1)} %bitcast.81, f32[512]{0:T(512)S(1)} %bitcast.84, f32[512]{0:T(512)S(1)} %bitcast.79, f32[512]{0:T(512)S(1)} %bitcast.82), kind=kLoop, calls=%fused_computation.41 | loop fusion | flops 1835008 | bytes 1060864 | tf_op jit(solution)/shard_map/convert
  45.1 1.5 %fusion.19 = f32[1024,256]{1,0:T(8,128)} fusion(bf16[512,512]{1,0:T(8,128)(2,1)S(1)} %get-tuple-element.98, bf16[512,512]{1,0:T(8,128)(2,1)S(1)} %get-tuple-element.97, f32[512,256]{1,0:T(8,128)S(1)} %all_gather.7, f32[512]{0:T(512)S(1)} %fusion.36), kind=kOutput, calls=%fused_computation.44 | convolution fusion | flops 270794752 | bytes 2623488 | tf_op jit(solution)/shard_map/dot_general | solution.py:64
  46.7 0.6 copy-done.6
  47.6 0.8 copy.13
  48.4 0.6 pad_maximum_fusion.6
  49.2 0.8 copy-done.4
  50.0 22.4 %while.10 = (s32[]{:T(128)}, f32[2,512,256]{2,1,0:T(8,128)S(1)}, s32[]{:T(128)}, s32[3,4]{1,0:T(4,128)S(1)}, s32[]{:T(128)}, /*index=5*/f32[3,128]{1,0:T(4,128)S...) while((s32[]{:T(128)}, f32[2,512,256]{2,1,0:T(8,128)S(1)}, ...), condition=%wide.region_1.2_spmd, body=%wide.region_0.1_spmd.sunk | while | flops 273989664 | bytes 1553877 | solution.py:111
  50.7 0.7 constant_dynamic-slice_fusion.6
  54.4 0.7 constant_dynamic-slice_fusion.7
  55.1 1.0 add_sqrt_fusion.2
  56.1 0.7 fusion.53
  56.8 0.5 fusion.54
  58.0 0.7 constant_dynamic-slice_fusion.6
  61.7 0.7 constant_dynamic-slice_fusion.7
  62.4 1.0 add_sqrt_fusion.2
  63.4 0.7 fusion.53
  64.0 0.5 fusion.54
  65.2 0.7 constant_dynamic-slice_fusion.6
  68.9 0.7 constant_dynamic-slice_fusion.7
  69.6 1.0 add_sqrt_fusion.2
  70.6 0.7 fusion.53
  71.3 0.5 fusion.54
  72.5 4.0 %collective-permute-start.2 = (f32[512,256]{1,0:T(8,128)S(1)}, f32[512,256]{1,0:T(8,128)}, u32[]{:S(2)}, u32[]{:S(2)}) collective-permute-start(f32[512,256]{1,0:T(8,128)S(1)} %slice_bitcast_fusion.6), channel_id=1, source_target_pairs={{0,4},{4,8},{8,12},{12,16},{16,20},{20,24},{24,28},{1,5},{5,9},{9,... | collective-permute-start | bytes 1572872 | tf_op jit(solution)/shard_map/ppermute | solution.py:17
  76.5 32.7 %all-reduce.2.cloned.1.call-done = f32[1024,256]{1,0:T(8,128)} async-done(((f32[1024,256]{1,0:T(8,128)}), f32[1024,256]{1,0:T(8,128)}) %all-reduce.2.cloned.1.call-update) | async-done | bytes 1048592 | tf_op jit(solution)/shard_map/psum | solution.py:65
  109.2 2.7 %fusion.21 = f32[512,256]{1,0:T(8,128)} fusion(f32[512,256]{1,0:T(8,128)} %collective-permute-done.2, f32[1024,256]{1,0:T(8,128)} %all-reduce.2.cloned.1.call-done, f32[512,256]{1,0:T(8,128)S(1)} %copy-done.7, bf16[512,512]{1,0:T(8,128)(2,1)S(1)} %copy-done.2, bf16[512,512]{1,0:T(8,128)(2,1)S(1)} %get-tuple-element.97, f32[2,512,256]{2,1,0:T(8,128)S(1)} %get-tuple-element.63), kind=kOutput, calls=%fused_computation.46 | convolution fusion | flops 271843328 | bytes 4194304 | tf_op jit(solution)/shard_map/dot_general | solution.py:70
  112.0 21.1 %reduce-scatter.2.cloned.1.call-done = f32[128,256]{1,0:T(8,128)} async-done(((f32[512,256]{1,0:T(8,128)}), f32[128,256]{1,0:T(8,128)}) %reduce-scatter.2.cloned.1.call-update) | async-done | bytes 131088 | tf_op jit(solution)/shard_map/reduce_scatter | solution.py:113
  133.2 1.9 %fusion.15 = f32[128,256]{1,0:T(8,128)} fusion(f32[128,256]{1,0:T(8,128)S(1)} %get-tuple-element.258, bf16[512,256]{1,0:T(8,128)(2,1)S(1)} %copy-done, bf16[256,512]{1,0:T(8,128)(2,1)S(1)} %copy-done.8, f32[128,256]{1,0:T(8,128)} %reduce-scatter.2.cloned.1.call-done, f32[128]{0:T(128)S(1)} %dynamic_slice.27), kind=kOutput, calls=%fused_computation.34 | convolution fusion | flops 67534848 | bytes 918016 | tf_op jit(solution)/shard_map/dot_general | solution.py:121
  (44 shorter events, 0.8 us)
Async XLA Ops:
  6.5 126.6 %copy-start = (bf16[512,256]{1,0:T(8,128)(2,1)S(1)}, bf16[512,256]{1,0:T(8,128)(2,1)}, u32[]{:S(2)}) copy-start(bf16[512,256]{1,0:T(8,128)(2,1)} %param.23) | copy-start | bytes 786436
  6.5 102.6 %all-reduce.2.cloned.1.call-start = ((), (), s32[]{:S(2)}) async-start(), calls=%async_computation.1 | async-start | bytes 2097152 | tf_op jit(solution)/shard_map/psum | solution.py:65
  20.4 28.0 %collective-permute-start = (f32[3,512]{1,0:T(4,128)S(1)}, f32[3,512]{1,0:T(4,128)S(1)}, u32[]{:S(2)}, u32[]{:S(2)}) collective-permute-start(f32[3,512]{1,0:T(4,128)S(1)} %all_gather.6), channel_id=1, source_target_pairs={{4,0},{8,4},{12,8},{16,12},{20,16},{24,20},{28,24},{5,1},{9,5},{13... | collective-permute-start | bytes 18440 | tf_op jit(solution)/shard_map/ppermute | solution.py:17
  37.8 11.2 %collective-permute-start.1 = (f32[512,256]{1,0:T(8,128)S(1)}, f32[512,256]{1,0:T(8,128)S(1)}, u32[]{:S(2)}, u32[]{:S(2)}) collective-permute-start(f32[512,256]{1,0:T(8,128)S(1)} %all_gather.7), channel_id=1, source_target_pairs={{4,0},{8,4},{12,8},{16,12},{20,16},{24,20},{28,24},{5,1},{9,5},{13... | collective-permute-start | bytes 1572872 | tf_op jit(solution)/shard_map/ppermute | solution.py:17
  44.4 2.2 %copy-start.1 = (bf16[512,512]{1,0:T(8,128)(2,1)}, bf16[512,512]{1,0:T(8,128)(2,1)S(1)}, u32[]{:S(2)}) copy-start(bf16[512,512]{1,0:T(8,128)(2,1)S(1)} %get-tuple-element.98) | copy-start | bytes 1572868
  46.6 0.7 copy-start.6
  46.6 1.0 copy-start.3
  46.6 86.5 %reduce-scatter.2.cloned.1.call-start = ((), (), s32[]{:S(2)}) async-start(), calls=%async_computation.2 | async-start | bytes 655360 | tf_op jit(solution)/shard_map/reduce_scatter | solution.py:113
  49.1 0.9 copy-start.4
  49.1 0.9 copy-start.5
  49.1 0.9 copy-start.9
  72.5 36.7 %copy-start.2 = (bf16[512,512]{1,0:T(8,128)(2,1)S(1)}, bf16[512,512]{1,0:T(8,128)(2,1)}, u32[]{:S(2)}) copy-start(bf16[512,512]{1,0:T(8,128)(2,1)} %copy-done.1) | copy-start | bytes 1572868
  72.5 36.7 %copy-start.7 = (f32[512,256]{1,0:T(8,128)S(1)}, f32[512,256]{1,0:T(8,128)}, u32[]{:S(2)}) copy-start(f32[512,256]{1,0:T(8,128)} %param.21) | copy-start | bytes 1572868
  72.5 36.7 %collective-permute-start.2 = (f32[512,256]{1,0:T(8,128)S(1)}, f32[512,256]{1,0:T(8,128)}, u32[]{:S(2)}, u32[]{:S(2)}) collective-permute-start(f32[512,256]{1,0:T(8,128)S(1)} %slice_bitcast_fusion.6), channel_id=1, source_target_pairs={{0,4},{4,8},{8,12},{12,16},{16,20},{20,24},{24,28},{1,5},{5,9},{9,... | collective-permute-start | bytes 1572872 | tf_op jit(solution)/shard_map/ppermute | solution.py:17
  109.2 24.0 %copy-start.8 = (bf16[256,512]{1,0:T(8,128)(2,1)S(1)}, bf16[256,512]{1,0:T(8,128)(2,1)}, u32[]{:S(2)}) copy-start(bf16[256,512]{1,0:T(8,128)(2,1)} %param.22) | copy-start | bytes 786436
Sparse Core Ops, SparseCore 0:
  46.8 62.3 all-reduce.1
  112.0 21.0 reduce-scatter.1
where the time goes:
time: 143 us; the launch traced here: 142 us
  waiting for transfers between devices  53.9 us (38%)
  blocking collectives  30 us (21%)
  between operations  14.2 us (10%)
  loops' own time  11.8 us (8%)
  matrix products  9.66 us (7%)
  other arithmetic  8.1 us (6%)
  local copies, waits for them, and re-layouts  7.73 us (5%)
  starting transfers between devices  6.57 us (5%)
    psum x1, waiting for transfers between devices, local(): factors = lax.psum(partial_value, 'wide')  32.7 us
    reduce_scatter x1, waiting for transfers between devices, local(): lax.psum_scatter(buffers[0] + arrived + long_part, 'narrow', scatter_dime...  21.1 us
    all_gather x1, blocking collectives, local(): lax.all_gather(features, 'narrow', axis=0, tiled=True)  16.1 us
    all_gather x1, blocking collectives, local(): lax.all_gather(positions, 'narrow', axis=1, tiled=True)  13.9 us
    another operation x1, loops' own time, local(): lax.fori_loop(0, listed, add_pair, jnp.zeros((2, slab_atoms, channels), j...  11.8 us
    ppermute x3, starting transfers between devices, from_behind(): return lax.ppermute(shard, axis, pairs)  6.53 us
    another operation x1, other arithmetic  4.46 us
    sqrt x3, other arithmetic, radial_filters(): distance = jnp.sqrt(squared + 0.01)  2.93 us
  transfers between devices with their start and end apart: 5, of which 2 were waited for; matrix products, arithmetic and copies ran while one was open for 13% of the time, Pallas kernels for 0%

commit v1 on v0

v1 whole, which is shorter than its diff:
```python
import functools
import math

import jax
import jax.numpy as jnp
from jax import lax
from jax.experimental import pallas as pl
from jax.experimental.pallas import tpu as pltpu
from jax.sharding import PartitionSpec as P

cutoff = 2.0
sigma_width = 0.25
MESH = pl.DeviceIdType.MESH
f32, bf16 = jnp.float32, jnp.bfloat16

COS = (1.0, -19.73920440673828, 64.93911743164062, -85.45014190673828,
       60.167633056640625, -25.967601776123047, 6.528658866882324)
SIN = (6.2831854820251465, -41.34170150756836, 81.60513305664062, -76.70301818847656,
       42.02592849731445, -14.899847984313965, 3.238137722015381)


def horner(coefs, u):
    acc = coefs[-1]
    for c in coefs[-2::-1]:
        acc = acc * u + c
    return acc


def column(row, size):
    return jnp.transpose(jnp.broadcast_to(row, (size, size)))


def kernel(
    cfg,
    pos_ref, cnt_ref, list_ref, pcount_ref, wrbf_ref, wv_ref,
    feat_ref, mask_hbm, kf_hbm, win_hbm, wout_hbm,
    out_ref,
    both, bpos, table, table_t, fact, rbuf, gath, filt,
    gh, gt, yown, ypeer, tp, buf, own_acc, ncv, msg, msum, sb, fin,
    mask, kf, win, wout,
    lsem, psend, precv, fsend, frecv, nsend, nrecv, npsend, nprecv,
    asend, arecv, zsend, zrecv, msend, mrecv, esend, erecv,
):
    W, N, B, C, RBF, SLOTS = cfg
    w, n = lax.axis_index("wide"), lax.axis_index("narrow")
    bits = W.bit_length() - 1
    qdev = wv_ref.shape[1]
    rows = 2 * qdev

    locals_ = [
        pltpu.make_async_copy(feat_ref, both.at[n], lsem.at[0]),
        pltpu.make_async_copy(mask_hbm.at[0, 0], mask, lsem.at[1]),
        pltpu.make_async_copy(kf_hbm, kf, lsem.at[2]),
        pltpu.make_async_copy(win_hbm, win, lsem.at[3]),
        pltpu.make_async_copy(wout_hbm, wout, lsem.at[4]),
    ]
    for copy in locals_:
        copy.start()
    bpos[n] = pos_ref[...]

    barrier = pltpu.get_barrier_semaphore()
    partners = [dict(wide=w, narrow=lax.rem(n + d, N)) for d in range(1, N)]
    partners += [dict(wide=w + (1 - 2 * ((w // (1 << b)) % 2)) * (1 << b), narrow=n) for b in range(bits)]
    partners += [dict(wide=lax.rem(w + 1, W), narrow=n), dict(wide=lax.rem(w + W - 1, W), narrow=n)]
    for p in partners:
        pl.semaphore_signal(barrier, inc=1, device_id=p, device_id_type=MESH)
    pl.semaphore_wait(barrier, len(partners))

    def to(src, dst, ss, rs, **dev):
        ids = dict(wide=w, narrow=n)
        ids.update(dev)
        return pltpu.make_async_remote_copy(
            src_ref=src, dst_ref=dst, send_sem=ss, recv_sem=rs, device_id=ids, device_id_type=MESH
        )

    has_prev = w > 0
    has_next = w < W - 1
    prev = lax.rem(w + W - 1, W)
    nxt = lax.rem(w + 1, W)

    pos_out, feat_out = [], []
    for d in range(1, N):
        pos_out.append(to(pos_ref, bpos.at[n], psend.at[d], precv.at[d], narrow=lax.rem(n + d, N)))
        pos_out[-1].start()
    for d in (2, 1, 3) if N == 4 else range(1, N):
        feat_out.append(to(feat_ref, both.at[n], fsend.at[d], frecv.at[d], narrow=lax.rem(n + d, N)))
        feat_out[-1].start()

    def forward(i, j):
        return to(both.at[j], both.at[N + j], nsend.at[i], nrecv.at[i], wide=prev)

    locals_[0].wait()

    @pl.when(has_prev)
    def _():
        forward(0, n).start()

    for d in range(1, N):
        src = lax.rem(n + N - d, N)
        to(pos_ref, bpos.at[src], psend.at[d], precv.at[d], narrow=src).wait_recv()
    pos_fwd = to(bpos.at[pl.ds(0, N)], bpos.at[pl.ds(N, N)], npsend, nprecv, wide=prev)

    @pl.when(has_prev)
    def _():
        pos_fwd.start()

    def wave_chunk(qc, _):
        q0 = pl.multiple_of(qc * B, B)
        wc = [column(wv_ref[i : i + 1, pl.ds(q0, B)] * (0.5 / math.pi), B) for i in range(3)]

        def atom_chunk(j, _):
            p = bpos[j]
            t = wc[0] * p[0:1] + wc[1] * p[1:2] + wc[2] * p[2:3]
            t = t - jnp.round(t)
            u = t * t
            for base, value in ((0, horner(COS, u)), (qdev, t * horner(SIN, u))):
                at = pl.multiple_of(base + q0, B)
                table[pl.ds(at, B), pl.ds(pl.multiple_of(j * B, B), B)] = value.astype(bf16)
                table_t[j, :, pl.ds(at, B)] = jnp.transpose(value).astype(bf16)
            return 0

        return lax.fori_loop(0, N, atom_chunk, 0)

    lax.fori_loop(0, qdev // B, wave_chunk, 0)

    f_own = both[n]
    for k in range(RBF):
        yown[k * B : (k + 1) * B, :] = (f_own * wrbf_ref[k : k + 1, :]).astype(bf16)

    @pl.when(has_next)
    def _():
        to(bpos.at[pl.ds(0, N)], bpos.at[pl.ds(N, N)], npsend, nprecv, wide=prev).wait_recv()

    @pl.when(jnp.logical_not(has_next))
    def _():
        bpos[pl.ds(N, N)] = jnp.zeros((N,) + bpos.shape[1:], f32)

    locals_[1].wait()
    alpha = math.sqrt(math.log2(math.e)) / sigma_width
    for i in range(3):
        ncv[i] = column(pos_ref[i : i + 1, :], B)

    def slot_filters(s, _):
        p = bpos[list_ref[0, 0, 1, s] * N + list_ref[0, 0, 2, s]]
        taken = jnp.where(s < pcount_ref[0, 0], 1.0, 0.0).astype(f32)
        dx, dy, dz = ncv[0] - p[0:1], ncv[1] - p[1:2], ncv[2] - p[2:3]
        squared = dx * dx + dy * dy + dz * dz
        dist = jnp.sqrt(squared + 0.01) * alpha
        env = 1.0 - jnp.minimum(squared * (1.0 / (cutoff * cutoff)), 1.0)
        em = env * env * (mask[s].astype(f32) * taken)
        dist_t, em_t = jnp.transpose(dist), jnp.transpose(em)
        for k in range(RBF):
            center = k * (cutoff / (RBF - 1)) * alpha
            a = dist - center
            b = dist_t - center
            gh[s, :, k * B : (k + 1) * B] = (jnp.exp2(-(a * a)) * em).astype(bf16)
            gt[s, :, k * B : (k + 1) * B] = (jnp.exp2(-(b * b)) * em_t).astype(bf16)
        return 0

    lax.fori_loop(0, SLOTS, slot_filters, 0)

    for s in range(SLOTS):
        tp[s] = jnp.dot(gt[s], yown[...], preferred_element_type=f32)

    def spread(j, _):
        acc = jnp.zeros((B, C), f32)
        for s in range(SLOTS):
            hit = (list_ref[0, 0, 1, s] * N + list_ref[0, 0, 2, s]) == j
            acc = acc + tp[s] * jnp.where(hit, 1.0, 0.0).astype(f32)
        buf[j] = acc
        return 0

    lax.fori_loop(0, 2 * N, spread, 0)

    live = cnt_ref[0]

    def weight(j):
        return jnp.where(j < live, 1.0, 0.0).astype(f32)

    for i, d in enumerate((1, 2, 3) if N == 4 else range(1, N)):
        src = lax.rem(n + N - d, N)
        to(feat_ref, both.at[src], fsend.at[d], frecv.at[d], narrow=src).wait_recv()

        @pl.when(has_prev)
        def _():
            forward(d, src).start()

    weighted = jnp.concatenate([(both[j] * weight(j)).astype(bf16) for j in range(N)], axis=0)

    nh = 2 if (rows // 2) % (8 * W) == 0 else 1
    hrows = rows // nh
    orders = [list(range(bits)), [0] + list(range(bits - 1, 0, -1))][:nh]

    def bit_of(b):
        return (w // (1 << b)) % 2

    def partner(b):
        return w + (1 - 2 * bit_of(b)) * (1 << b)

    state = [dict(off=h * hrows, size=hrows, at=h * hrows) for h in range(nh)]
    pending = []

    def mult8(x):
        return pl.multiple_of(x, 8)

    def rs_start(h, s):
        st, b = state[h], orders[h][s]
        half = st["size"] // 2
        mine = st["off"] + bit_of(b) * half
        other = st["off"] + (1 - bit_of(b)) * half
        i = h * 2 * bits + s
        copy = to(fact.at[pl.ds(mult8(other), half)], rbuf.at[pl.ds(st["at"], half)], asend.at[i], arecv.at[i], wide=partner(b))
        copy.start()
        pending.append(copy)
        st.update(copy=copy, off=mine, size=half)

    def rs_finish(h, s):
        st = state[h]
        st["copy"].wait_recv()
        part = pl.ds(mult8(st["off"]), st["size"])
        total = fact[part, :] + rbuf[pl.ds(st["at"], st["size"]), :]
        st["at"] += st["size"]
        if s == bits - 1:
            gath[part, :] = total
        else:
            fact[part, :] = total

    def ag_start(h, s):
        st, b = state[h], orders[h][s]
        part = pl.ds(mult8(st["off"]), st["size"])
        i = h * 2 * bits + bits + s
        copy = to(gath.at[part], gath.at[part], asend.at[i], arecv.at[i], wide=partner(b))
        copy.start()
        pending.append(copy)

    def ag_finish(h, s):
        st, b = state[h], orders[h][s]
        i = h * 2 * bits + bits + s
        there = st["off"] + (1 - 2 * bit_of(b)) * st["size"]
        part = pl.ds(mult8(there), st["size"])
        to(gath.at[part], gath.at[part], asend.at[i], arecv.at[i], wide=partner(b)).wait_recv()
        st.update(off=st["off"] - bit_of(b) * st["size"], size=st["size"] * 2)

    step = min(hrows, 256)
    for h in range(nh):
        for r in range(h * hrows, (h + 1) * hrows, step):
            fact[r : r + step, :] = jnp.dot(table[r : r + step, :], weighted, preferred_element_type=f32)
        rs_start(h, 0)

    znext = []
    for d in range(1, N):
        j = lax.rem(n + d, N)
        znext.append(to(buf.at[N + j], sb.at[d], zsend.at[d], zrecv.at[d], narrow=j))
        znext[-1].start()

    def job_peer(s):
        def run():
            if s == 0:
                for i in range(N):
                    j = lax.rem(n + N - i, N)

                    @pl.when(has_next)
                    def _():
                        forward(i, j).wait_recv()

                @pl.when(jnp.logical_not(has_next))
                def _():
                    for i in range(N):
                        both[N + i] = jnp.zeros((B, C), f32)

            f_peer = both[list_ref[0, 0, 1, s] * N + list_ref[0, 0, 2, s]]
            for k in range(RBF):
                ypeer[k * B : (k + 1) * B, :] = (f_peer * wrbf_ref[k : k + 1, :]).astype(bf16)
            value = jnp.dot(gh[s], ypeer[...], preferred_element_type=f32)
            own_acc[...] = value if s == 0 else own_acc[...] + value

        return run

    def job_next():
        for copy in znext:
            copy.wait_recv()
        msum[...] = buf[N + n] + sb[1] + sb[2] + sb[3] if N == 4 else sum((sb[d] for d in range(1, N)), buf[N + n])

        @pl.when(has_next)
        def _():
            to(msum, msg, msend, mrecv, wide=nxt).start()

    jobs = [job_peer(s) for s in range(SLOTS)]
    jobs.insert(min(2, len(jobs)), job_next)
    for s in range(2 * bits):
        if jobs:
            jobs.pop(0)()
        for h in range(nh):
            if s < bits:
                rs_finish(h, s)
                if s < bits - 1:
                    rs_start(h, s + 1)
                else:
                    ag_start(h, bits - 1)
            else:
                a = 2 * bits - 1 - s
                ag_finish(h, a)
                if a > 0:
                    ag_start(h, a - 1)
    for job in jobs:
        job()

    atoms_all = B * N * W
    locals_[2].wait()
    for base in (0, qdev):
        filt[base : base + qdev, :] = (kf[...] * gath[base : base + qdev, :] / atoms_all).astype(bf16)

    last = []
    for d in (2, 1, 3) if N == 4 else range(1, N):
        j = lax.rem(n + d, N)
        fin[d] = buf[j] + jnp.dot(table_t[j], filt[...], preferred_element_type=f32)
        last.append(to(fin.at[d], fin.at[N + d], esend.at[d], erecv.at[d], narrow=j))
        last[-1].start()
    own = buf[n] + own_acc[...] + jnp.dot(table_t[n], filt[...], preferred_element_type=f32)

    @pl.when(has_prev)
    def _():
        to(msum, msg, msend, mrecv, wide=nxt).wait_recv()

    @pl.when(jnp.logical_not(has_prev))
    def _():
        msg[...] = jnp.zeros_like(msg)

    own = own + msg[...]
    locals_[3].wait()
    locals_[4].wait()
    for copy in last:
        copy.wait_recv()
    for d in range(1, N):
        own = own + fin[N + d]
    hidden = jnp.dot(own.astype(bf16), win[...], preferred_element_type=f32)
    hidden = (hidden / (1.0 + jnp.exp(-hidden))).astype(bf16)
    out_ref[...] = weight(n) * (both[n] + jnp.dot(hidden, wout[...], preferred_element_type=f32))

    for copy in pos_out + feat_out + znext + last + pending:
        copy.wait_send()

    @pl.when(has_prev)
    def _():
        pos_fwd.wait_send()
        for i in range(N):
            forward(i, lax.rem(n + N - i, N)).wait_send()

    @pl.when(has_next)
    def _():
        to(msum, msg, msend, mrecv, wide=nxt).wait_send()


def local(W, N, positions, features, block_counts, pair_list, pair_count, pair_mask, w_rbf, wavevectors, kfilter, w_in, w_out):
    B, C = features.shape
    RBF = w_rbf.shape[0]
    SLOTS = pair_list.shape[3]
    rows = 2 * wavevectors.shape[1]
    bits = W.bit_length() - 1
    vmem = pl.BlockSpec(memory_space=pltpu.VMEM)
    smem = pl.BlockSpec(memory_space=pltpu.SMEM)
    hbm = pl.BlockSpec(memory_space=pl.ANY)
    dma = pltpu.SemaphoreType.DMA
    V = pltpu.VMEM
    return pl.pallas_call(
        functools.partial(kernel, (W, N, B, C, RBF, SLOTS)),
        out_shape=jax.ShapeDtypeStruct((B, C), f32),
        in_specs=[vmem, smem, smem, smem, vmem, vmem, hbm, hbm, hbm, hbm, hbm],
        out_specs=vmem,
        scratch_shapes=[
            V((2 * N, B, C), f32),
            V((2 * N, 3, B), f32),
            V((rows, N * B), bf16),
            V((N, B, rows), bf16),
            V((rows, C), f32),
            V((rows, C), f32),
            V((rows, C), f32),
            V((rows, C), bf16),
            V((SLOTS, B, RBF * B), bf16),
            V((SLOTS, B, RBF * B), bf16),
            V((RBF * B, C), bf16),
            V((RBF * B, C), bf16),
            V((SLOTS, B, C), f32),
            V((2 * N, B, C), f32),
            V((B, C), f32),
            V((3, B, B), f32),
            V((B, C), f32),
            V((B, C), f32),
            V((N, B, C), f32),
            V((2 * N, B, C), f32),
            V(pair_mask.shape[2:], jnp.int32),
            V(kfilter.shape, f32),
            V(w_in.shape, bf16),
            V(w_out.shape, bf16),
            dma((5,)),
            dma((N,)), dma((N,)),
            dma((N,)), dma((N,)),
            dma((N,)), dma((N,)),
            dma, dma,
            dma((4 * bits,)), dma((4 * bits,)),
            dma((N,)), dma((N,)),
            dma, dma,
            dma((N,)), dma((N,)),
        ],
        compiler_params=pltpu.CompilerParams(
            collective_id=0, has_side_effects=True, vmem_limit_bytes=48 << 20
        ),
    )(positions, block_counts, pair_list, pair_count, w_rbf, wavevectors, features, pair_mask, kfilter, w_in, w_out)


def solution(mesh):
    placed = (
        P(None, ("wide", "narrow")),
        P(("wide", "narrow"), None),
        P("wide"),
        P("wide", "narrow", None, None),
        P("wide", "narrow"),
        P("wide", "narrow", None, None, None),
        P(),
        P(None, "narrow"),
        P("narrow", None),
        P(),
        P(),
    )
    body = functools.partial(local, mesh.shape["wide"], mesh.shape["narrow"])
    return jax.shard_map(
        body, mesh=mesh, in_specs=placed, out_specs=P(("wide", "narrow"), None), check_vma=False
    )
```

time: 143 us -> 63.4 us (0.44)
  Pallas kernels: 0 us -> 53.9 us
  waiting for transfers between devices: 53.9 us -> 0 us
  blocking collectives: 30 us -> 0 us
  between operations: 14.2 us -> 1.35 us
  loops' own time: 11.8 us -> 0 us
  matrix products: 9.66 us -> 0 us
  other arithmetic: 8.1 us -> 0 us
  starting transfers between devices: 6.57 us -> 0 us
    pallas_call x0 -> x1, Pallas kernels: none -> 53.9 us  [local(): pl.pallas_call(functools.partial(kernel, (W, N, B, C, RBF, SLOTS)), out_s...]
    psum x1 -> x0, waiting for transfers between devices: 32.7 us -> none  [local(): factors = lax.psum(partial_value, 'wide')]
    all_gather x2 -> x0, blocking collectives: 30 us -> none  [the longest x1 16.1 us: local(): lax.all_gather(features, 'narrow', axis=0, tiled=True)]
    reduce_scatter x1 -> x0, waiting for transfers between devices: 21.1 us -> none  [local(): lax.psum_scatter(buffers[0] + arrived + long_part, 'narrow', scatter_dime...]
    another operation x1 -> x0, loops' own time: 11.8 us -> none  [local(): lax.fori_loop(0, listed, add_pair, jnp.zeros((2, slab_atoms, channels), j...]
    dot_general x9 -> x0, matrix products: 9.66 us -> none  [the longest x1 2.71 us: local(): lax.dot_general(tables, filtered, (((0,), (0,)), ((), ())), preferred_ele...]
    ppermute x3 -> x0, starting transfers between devices: 6.53 us -> none  [from_behind(): return lax.ppermute(shard, axis, pairs)]
    another operation x3 -> x0, other arithmetic: 5.14 us -> none
  transfers between devices with their start and end apart: 5 -> 0, of which waited for: 2 -> 0; matrix products, arithmetic and copies ran while one was open for 13% -> 0% of each run, Pallas kernels for 0% -> 0%
where the time goes in v1:
time: 63.4 us; the launch traced here: 62.8 us
  Pallas kernels  53.9 us (85%)
  local copies, waits for them, and re-layouts  7.53 us (12%)
  between operations  1.35 us (2%)
    pallas_call x1, Pallas kernels, local(): pl.pallas_call(functools.partial(kernel, (W, N, B, C, RBF, SLOTS)), out_s...  53.9 us
    unnamed x20, local copies, waits for them, and re-layouts  7.53 us

profile of v1, /device:TPU:0, one launch (start us, length us, event | category | flops | bytes accessed | tf_op | source)
XLA Modules:
  0.0 62.8 jit_solution(16849809923285513971)
XLA Ops:
  0.0 0.0 copy-start.8
  1.3 0.0 copy-done.8
  1.3 0.0 copy-start.7
  1.3 0.7 %copy-done.7 = f32[3,128]{1,0:T(4,128)S(1)} copy-done((f32[3,128]{1,0:T(4,128)S(1)}, f32[3,128]{1,0:T(4,128)}, u32[]{:S(2)}) %copy-start.7) | copy-done | bytes 1560
  2.0 0.0 copy-start
  2.0 1.0 %copy-done = f32[512,256]{1,0:T(8,128)S(1)} copy-done((f32[512,256]{1,0:T(8,128)S(1)}, f32[512,256]{1,0:T(8,128)}, u32[]{:S(2)}) %copy-start) | copy-done | bytes 524312
  3.0 0.0 copy-start.1
  3.1 0.9 %copy-done.1 = s32[1,1,4,128,128]{4,3,2,1,0:T(8,128)S(1)} copy-done((s32[1,1,4,128,128]{4,3,2,1,0:T(8,128)S(1)}, s32[1,1,4,128,128]{4,3,2,1,0:T(8,128)}, u32[]{:S(2)}) %copy-start.1) | copy-done | bytes 262168
  4.0 0.0 copy-start.2
  4.0 0.9 %copy-done.2 = bf16[256,512]{1,0:T(8,128)(2,1)S(1)} copy-done((bf16[256,512]{1,0:T(8,128)(2,1)S(1)}, bf16[256,512]{1,0:T(8,128)(2,1)}, u32[]{:S(2)}) %copy-start.2) | copy-done | bytes 262168
  5.0 0.0 copy-start.3
  5.0 0.9 %copy-done.3 = bf16[512,256]{1,0:T(8,128)(2,1)S(1)} copy-done((bf16[512,256]{1,0:T(8,128)(2,1)S(1)}, bf16[512,256]{1,0:T(8,128)(2,1)}, u32[]{:S(2)}) %copy-start.3) | copy-done | bytes 262168
  5.9 0.0 copy-start.4
  5.9 0.9 %copy-done.4 = f32[128,256]{1,0:T(8,128)S(1)} copy-done((f32[128,256]{1,0:T(8,128)S(1)}, f32[128,256]{1,0:T(8,128)}, u32[]{:S(2)}) %copy-start.4) | copy-done | bytes 131096
  6.8 0.0 copy-start.5
  6.8 0.7 %copy-done.5 = f32[16,256]{1,0:T(8,128)S(1)} copy-done((f32[16,256]{1,0:T(8,128)S(1)}, f32[16,256]{1,0:T(8,128)}, u32[]{:S(2)}) %copy-start.5) | copy-done | bytes 16408
  7.5 0.0 copy-start.6
  7.5 0.7 %copy-done.6 = f32[3,512]{1,0:T(4,128)S(1)} copy-done((f32[3,512]{1,0:T(4,128)S(1)}, f32[3,512]{1,0:T(4,128)}, u32[]{:S(2)}) %copy-start.6) | copy-done | bytes 6168
  8.2 53.9 %shard_map.109 = f32[128,256]{1,0:T(8,128)S(1)} custom-call(f32[3,128]{1,0:T(4,128)S(1)} %copy-done.7, s32[1]{0:T(128)S(6)} %copy.14.cnt_ref, s32[1,1,3,4]{3,2,1,0:T(4,128)S(1)} %copy.12.list_ref, s32[1,1]{1,0:T(1,128)S(6)} %copy.15.pcount_ref, f32[16,256]{1,0:T(8,128)S(1)} %copy-done.5, f32[3,512]{1,0:T(4,128)S(1)} %copy-done.6, f32[128,256]{1,0:T(8,128)S(1)} %copy-done.4, ...), custom_call_target="tpu_custom_call" | custom-call | tf_op jit(solution)/shard_map/pallas_call | solution.py:365
  62.1 0.7 %copy.16 = f32[128,256]{1,0:T(8,128)} copy(f32[128,256]{1,0:T(8,128)S(1)} %shard_map.109) | data formatting | bytes 262144
  (1 shorter events, 0.0 us)
Async XLA Ops:
  0.0 1.3 %copy-start.8 = (s32[1,1,3,4]{3,1,2,0:T(1,128)S(1)}, s32[1,1,3,4]{3,1,2,0:T(1,128)}, u32[]{:S(2)}) copy-start(s32[1,1,3,4]{3,1,2,0:T(1,128)} %param.14) | copy-start | bytes 148
  1.3 0.7 %copy-start.7 = (f32[3,128]{1,0:T(4,128)S(1)}, f32[3,128]{1,0:T(4,128)}, u32[]{:S(2)}) copy-start(f32[3,128]{1,0:T(4,128)} %pos_ref.1) | copy-start | bytes 4612
  2.0 1.0 %copy-start = (f32[512,256]{1,0:T(8,128)S(1)}, f32[512,256]{1,0:T(8,128)}, u32[]{:S(2)}) copy-start(f32[512,256]{1,0:T(8,128)} %kf_hbm.1) | copy-start | bytes 1572868
  3.0 0.9 %copy-start.1 = (s32[1,1,4,128,128]{4,3,2,1,0:T(8,128)S(1)}, s32[1,1,4,128,128]{4,3,2,1,0:T(8,128)}, u32[]{:S(2)}) copy-start(s32[1,1,4,128,128]{4,3,2,1,0:T(8,128)} %mask_hbm.1) | copy-start | bytes 786436
  4.0 0.9 %copy-start.2 = (bf16[256,512]{1,0:T(8,128)(2,1)S(1)}, bf16[256,512]{1,0:T(8,128)(2,1)}, u32[]{:S(2)}) copy-start(bf16[256,512]{1,0:T(8,128)(2,1)} %win_hbm.1) | copy-start | bytes 786436
  5.0 0.9 %copy-start.3 = (bf16[512,256]{1,0:T(8,128)(2,1)S(1)}, bf16[512,256]{1,0:T(8,128)(2,1)}, u32[]{:S(2)}) copy-start(bf16[512,256]{1,0:T(8,128)(2,1)} %wout_hbm.1) | copy-start | bytes 786436
  5.9 0.9 %copy-start.4 = (f32[128,256]{1,0:T(8,128)S(1)}, f32[128,256]{1,0:T(8,128)}, u32[]{:S(2)}) copy-start(f32[128,256]{1,0:T(8,128)} %feat_ref.1) | copy-start | bytes 393220
  6.8 0.7 %copy-start.5 = (f32[16,256]{1,0:T(8,128)S(1)}, f32[16,256]{1,0:T(8,128)}, u32[]{:S(2)}) copy-start(f32[16,256]{1,0:T(8,128)} %wrbf_ref.1) | copy-start | bytes 49156
  7.5 0.7 %copy-start.6 = (f32[3,512]{1,0:T(4,128)S(1)}, f32[3,512]{1,0:T(4,128)}, u32[]{:S(2)}) copy-start(f32[3,512]{1,0:T(4,128)} %wv_ref.1) | copy-start | bytes 18436

commit v2 on v1

--- a/solution.py
+++ b/solution.py
@@ -32,9 +32,10 @@
 
 def kernel(
     cfg,
-    pos_ref, cnt_ref, list_ref, pcount_ref, wrbf_ref, wv_ref,
-    feat_ref, mask_hbm, kf_hbm, win_hbm, wout_hbm,
+    cnt_ref, list_ref, pcount_ref,
+    pos_hbm, wrbf_hbm, wv_hbm, feat_ref, mask_hbm, kf_hbm, win_hbm, wout_hbm,
     out_ref,
+    pos_ref, wrbf_ref, wv_ref,
     both, bpos, table, table_t, fact, rbuf, gath, filt,
     gh, gt, yown, ypeer, tp, buf, own_acc, ncv, msg, msum, sb, fin,
     mask, kf, win, wout,
@@ -53,10 +54,13 @@
         pltpu.make_async_copy(kf_hbm, kf, lsem.at[2]),
         pltpu.make_async_copy(win_hbm, win, lsem.at[3]),
         pltpu.make_async_copy(wout_hbm, wout, lsem.at[4]),
+        pltpu.make_async_copy(pos_hbm, pos_ref, lsem.at[5]),
+        pltpu.make_async_copy(wrbf_hbm, wrbf_ref, lsem.at[6]),
+        pltpu.make_async_copy(wv_hbm, wv_ref, lsem.at[7]),
+        pltpu.make_async_copy(pos_hbm, bpos.at[n], lsem.at[8]),
     ]
-    for copy in locals_:
-        copy.start()
-    bpos[n] = pos_ref[...]
+    for i in (5, 8, 7, 0, 6, 1, 2, 3, 4):
+        locals_[i].start()
 
     barrier = pltpu.get_barrier_semaphore()
     partners = [dict(wide=w, narrow=lax.rem(n + d, N)) for d in range(1, N)]
@@ -80,7 +84,7 @@
 
     pos_out, feat_out = [], []
     for d in range(1, N):
-        pos_out.append(to(pos_ref, bpos.at[n], psend.at[d], precv.at[d], narrow=lax.rem(n + d, N)))
+        pos_out.append(to(pos_hbm, bpos.at[n], psend.at[d], precv.at[d], narrow=lax.rem(n + d, N)))
         pos_out[-1].start()
     for d in (2, 1, 3) if N == 4 else range(1, N):
         feat_out.append(to(feat_ref, both.at[n], fsend.at[d], frecv.at[d], narrow=lax.rem(n + d, N)))
@@ -89,7 +93,8 @@
     def forward(i, j):
         return to(both.at[j], both.at[N + j], nsend.at[i], nrecv.at[i], wide=prev)
 
-    locals_[0].wait()
+    for i in (0, 5, 6, 7, 8):
+        locals_[i].wait()
 
     @pl.when(has_prev)
     def _():
@@ -141,7 +146,7 @@
         ncv[i] = column(pos_ref[i : i + 1, :], B)
 
     def slot_filters(s, _):
-        p = bpos[list_ref[0, 0, 1, s] * N + list_ref[0, 0, 2, s]]
+        p = bpos[list_ref[0, 1, 0, s] * N + list_ref[0, 2, 0, s]]
         taken = jnp.where(s < pcount_ref[0, 0], 1.0, 0.0).astype(f32)
         dx, dy, dz = ncv[0] - p[0:1], ncv[1] - p[1:2], ncv[2] - p[2:3]
         squared = dx * dx + dy * dy + dz * dz
@@ -165,7 +170,7 @@
     def spread(j, _):
         acc = jnp.zeros((B, C), f32)
         for s in range(SLOTS):
-            hit = (list_ref[0, 0, 1, s] * N + list_ref[0, 0, 2, s]) == j
+            hit = (list_ref[0, 1, 0, s] * N + list_ref[0, 2, 0, s]) == j
             acc = acc + tp[s] * jnp.where(hit, 1.0, 0.0).astype(f32)
         buf[j] = acc
         return 0
@@ -268,7 +273,7 @@
                     for i in range(N):
                         both[N + i] = jnp.zeros((B, C), f32)
 
-            f_peer = both[list_ref[0, 0, 1, s] * N + list_ref[0, 0, 2, s]]
+            f_peer = both[list_ref[0, 1, 0, s] * N + list_ref[0, 2, 0, s]]
             for k in range(RBF):
                 ypeer[k * B : (k + 1) * B, :] = (f_peer * wrbf_ref[k : k + 1, :]).astype(bf16)
             value = jnp.dot(gh[s], ypeer[...], preferred_element_type=f32)
@@ -359,15 +364,18 @@
     bits = W.bit_length() - 1
     vmem = pl.BlockSpec(memory_space=pltpu.VMEM)
     smem = pl.BlockSpec(memory_space=pltpu.SMEM)
-    hbm = pl.BlockSpec(memory_space=pl.ANY)
+    hbm = pl.BlockSpec(memory_space=pltpu.HBM)
     dma = pltpu.SemaphoreType.DMA
     V = pltpu.VMEM
     return pl.pallas_call(
         functools.partial(kernel, (W, N, B, C, RBF, SLOTS)),
         out_shape=jax.ShapeDtypeStruct((B, C), f32),
-        in_specs=[vmem, smem, smem, smem, vmem, vmem, hbm, hbm, hbm, hbm, hbm],
+        in_specs=[smem] * 3 + [hbm] * 8,
         out_specs=vmem,
         scratch_shapes=[
+            V(positions.shape, f32),
+            V(w_rbf.shape, f32),
+            V(wavevectors.shape, f32),
             V((2 * N, B, C), f32),
             V((2 * N, 3, B), f32),
             V((rows, N * B), bf16),
@@ -392,7 +400,7 @@
             V(kfilter.shape, f32),
             V(w_in.shape, bf16),
             V(w_out.shape, bf16),
-            dma((5,)),
+            dma((9,)),
             dma((N,)), dma((N,)),
             dma((N,)), dma((N,)),
             dma((N,)), dma((N,)),
@@ -403,9 +411,9 @@
             dma((N,)), dma((N,)),
         ],
         compiler_params=pltpu.CompilerParams(
-            collective_id=0, has_side_effects=True, vmem_limit_bytes=48 << 20
+            collective_id=0, has_side_effects=True, vmem_limit_bytes=67043328
         ),
-    )(positions, block_counts, pair_list, pair_count, w_rbf, wavevectors, features, pair_mask, kfilter, w_in, w_out)
+    )(block_counts, jnp.transpose(pair_list, (0, 2, 1, 3)), pair_count, positions, w_rbf, wavevectors, features, pair_mask, kfilter, w_in, w_out)
 
 
 def solution(mesh):

time: 63.4 us -> 58 us (0.915)
  local copies, waits for them, and re-layouts: 7.53 us -> 1.57 us
  Pallas kernels: 53.9 us -> 54.7 us
    unnamed x20 -> x1, local copies, waits for them, and re-layouts: 7.53 us -> 1.57 us
    pallas_call x1, Pallas kernels: 53.9 us -> 54.7 us  [local(): pl.pallas_call(functools.partial(kernel, (W, N, B, C, RBF, SLOTS)), out_s...]
where the time goes in v2:
time: 58 us; the launch traced here: 57.6 us
  Pallas kernels  54.7 us (94%)
  local copies, waits for them, and re-layouts  1.57 us (3%)
  between operations  1.3 us (2%)
    pallas_call x1, Pallas kernels, local(): pl.pallas_call(functools.partial(kernel, (W, N, B, C, RBF, SLOTS)), out_s...  54.7 us
    unnamed x1, local copies, waits for them, and re-layouts  1.57 us

profile of v2, /device:TPU:0, one launch (start us, length us, event | category | flops | bytes accessed | tf_op | source)
XLA Modules:
  0.0 57.6 jit_solution(11411478339173844495)
XLA Ops:
  1.3 54.7 %shard_map.109 = f32[128,256]{1,0:T(8,128)} custom-call(s32[1]{0:T(128)S(6)} %copy.13.cnt_ref, s32[1,3,1,4]{3,2,1,0:T(1,128)} %bitcast.1, s32[1,1]{1,0:T(1,128)S(6)} %copy.14.pcount_ref, f32[3,128]{1,0:T(4,128)} %pos_hbm.1, f32[16,256]{1,0:T(8,128)} %wrbf_hbm.1, f32[3,512]{1,0:T(4,128)} %wv_hbm.1, f32[128,256]{1,0:T(8,128)} %feat_ref.1, ...), custom_call_target="tpu_custom_call" | custom-call | tf_op jit(solution)/shard_map/pallas_call | solution.py:370
  56.0 1.6 %copy.15 = f32[128,256]{1,0:T(8,128)} copy(f32[128,256]{1,0:T(8,128)} %shard_map.109) | data formatting | bytes 262144

commit v3 on v2

--- a/solution.py
+++ b/solution.py
@@ -11,6 +11,7 @@
 cutoff = 2.0
 sigma_width = 0.25
 MESH = pl.DeviceIdType.MESH
+CHAINS = (8, 4, 2, 1)
 f32, bf16 = jnp.float32, jnp.bfloat16
 
 COS = (1.0, -19.73920440673828, 64.93911743164062, -85.45014190673828,
@@ -177,6 +178,12 @@
 
     lax.fori_loop(0, 2 * N, spread, 0)
 
+    znext = []
+    for d in range(1, N):
+        j = lax.rem(n + d, N)
+        znext.append(to(buf.at[N + j], sb.at[d], zsend.at[d], zrecv.at[d], narrow=j))
+        znext[-1].start()
+
     live = cnt_ref[0]
 
     def weight(j):
@@ -192,9 +199,9 @@
 
     weighted = jnp.concatenate([(both[j] * weight(j)).astype(bf16) for j in range(N)], axis=0)
 
-    nh = 2 if (rows // 2) % (8 * W) == 0 else 1
+    nh = next(c for c in CHAINS if rows % (c * 8 * W) == 0)
     hrows = rows // nh
-    orders = [list(range(bits)), [0] + list(range(bits - 1, 0, -1))][:nh]
+    orders = [list(range(bits)) if h % 2 == 0 else [0] + list(range(bits - 1, 0, -1)) for h in range(nh)]
 
     def bit_of(b):
         return (w // (1 << b)) % 2
@@ -252,12 +259,6 @@
             fact[r : r + step, :] = jnp.dot(table[r : r + step, :], weighted, preferred_element_type=f32)
         rs_start(h, 0)
 
-    znext = []
-    for d in range(1, N):
-        j = lax.rem(n + d, N)
-        znext.append(to(buf.at[N + j], sb.at[d], zsend.at[d], zrecv.at[d], narrow=j))
-        znext[-1].start()
-
     def job_peer(s):
         def run():
             if s == 0:
@@ -291,7 +292,6 @@
             to(msum, msg, msend, mrecv, wide=nxt).start()
 
     jobs = [job_peer(s) for s in range(SLOTS)]
-    jobs.insert(min(2, len(jobs)), job_next)
     for s in range(2 * bits):
         if jobs:
             jobs.pop(0)()
@@ -309,6 +309,7 @@
                     ag_start(h, a - 1)
     for job in jobs:
         job()
+    job_next()
 
     atoms_all = B * N * W
     locals_[2].wait()
@@ -405,7 +406,7 @@
             dma((N,)), dma((N,)),
             dma((N,)), dma((N,)),
             dma, dma,
-            dma((4 * bits,)), dma((4 * bits,)),
+            dma((2 * bits * CHAINS[0],)), dma((2 * bits * CHAINS[0],)),
             dma((N,)), dma((N,)),
             dma, dma,
             dma((N,)), dma((N,)),

time: 58 us -> 56.3 us (0.971)
  Pallas kernels: 54.7 us -> 52.7 us
    pallas_call x1, Pallas kernels: 54.7 us -> 52.7 us  [local(): pl.pallas_call(functools.partial(kernel, (W, N, B, C, RBF, SLOTS)), out_s...]
where the time goes in v3:
time: 56.3 us; the launch traced here: 55.6 us
  Pallas kernels  52.7 us (94%)
  local copies, waits for them, and re-layouts  1.57 us (3%)
  between operations  1.3 us (2%)
    pallas_call x1, Pallas kernels, local(): pl.pallas_call(functools.partial(kernel, (W, N, B, C, RBF, SLOTS)), out_s...  52.7 us
    unnamed x1, local copies, waits for them, and re-layouts  1.57 us

profile of v3, /device:TPU:0, one launch (start us, length us, event | category | flops | bytes accessed | tf_op | source)
XLA Modules:
  0.0 55.6 jit_solution(6430687328437433197)
XLA Ops:
  1.3 52.7 %shard_map.109 = f32[128,256]{1,0:T(8,128)} custom-call(s32[1]{0:T(128)S(6)} %copy.13.cnt_ref, s32[1,3,1,4]{3,2,1,0:T(1,128)} %bitcast.1, s32[1,1]{1,0:T(1,128)S(6)} %copy.14.pcount_ref, f32[3,128]{1,0:T(4,128)} %pos_hbm.1, f32[16,256]{1,0:T(8,128)} %wrbf_hbm.1, f32[3,512]{1,0:T(4,128)} %wv_hbm.1, f32[128,256]{1,0:T(8,128)} %feat_ref.1, ...), custom_call_target="tpu_custom_call" | custom-call | tf_op jit(solution)/shard_map/pallas_call | solution.py:371
  54.0 1.6 %copy.15 = f32[128,256]{1,0:T(8,128)} copy(f32[128,256]{1,0:T(8,128)} %shard_map.109) | data formatting | bytes 262144

commit v4 on v3

--- a/solution.py
+++ b/solution.py
@@ -314,7 +314,7 @@
     atoms_all = B * N * W
     locals_[2].wait()
     for base in (0, qdev):
-        filt[base : base + qdev, :] = (kf[...] * gath[base : base + qdev, :] / atoms_all).astype(bf16)
+        filt[base : base + qdev, :] = (kf[...] * gath[base : base + qdev, :] * (1.0 / atoms_all)).astype(bf16)
 
     last = []
     for d in (2, 1, 3) if N == 4 else range(1, N):

time: 56.3 us -> 56.3 us (level)
  no operation moved by 1% of the time
where the time goes in v4:
time: 56.3 us; the launch traced here: 55.6 us
  Pallas kernels  52.7 us (94%)
  local copies, waits for them, and re-layouts  1.57 us (3%)
  between operations  1.3 us (2%)
    pallas_call x1, Pallas kernels, local(): pl.pallas_call(functools.partial(kernel, (W, N, B, C, RBF, SLOTS)), out_s...  52.7 us
    unnamed x1, local copies, waits for them, and re-layouts  1.57 us

profile of v4, /device:TPU:0, one launch (start us, length us, event | category | flops | bytes accessed | tf_op | source)
XLA Modules:
  0.0 55.6 jit_solution(6430687328437433197)
XLA Ops:
  1.3 52.7 %shard_map.109 = f32[128,256]{1,0:T(8,128)} custom-call(s32[1]{0:T(128)S(6)} %copy.13.cnt_ref, s32[1,3,1,4]{3,2,1,0:T(1,128)} %bitcast.1, s32[1,1]{1,0:T(1,128)S(6)} %copy.14.pcount_ref, f32[3,128]{1,0:T(4,128)} %pos_hbm.1, f32[16,256]{1,0:T(8,128)} %wrbf_hbm.1, f32[3,512]{1,0:T(4,128)} %wv_hbm.1, f32[128,256]{1,0:T(8,128)} %feat_ref.1, ...), custom_call_target="tpu_custom_call" | custom-call | tf_op jit(solution)/shard_map/pallas_call | solution.py:371
  54.0 1.6 %copy.15 = f32[128,256]{1,0:T(8,128)} copy(f32[128,256]{1,0:T(8,128)} %shard_map.109) | data formatting | bytes 262144
